TPU v7x, 256 devices: a whole 4x4x8 slice. The times are simulated.
256 devices in a mesh: tm: 64 (over y, z_hi, x), neur: 4 (over z_lo, core).
Axes of the slice: x: 4, y: 4, z: 8 (z_hi: 4, z_lo: 2; z = z_hi * 2 + z_lo), core: 2. Of those that a mesh axis runs over, the one named last changes fastest.
Arguments:
- recording: bfloat16 [2048, 16384], P('neur', 'tm'), may hold values from -6 to 6
- motifs: bfloat16 [128, 64, 2048], P(None, None, 'neur'), may hold values from -0.0625 to 0.0625
- loadings: bfloat16 [64, 16384], P(None, 'tm'), may hold values from -6 to 6
Outputs:
- grad_motifs: float32 [128, 64, 2048], P('tm', None, 'neur')
- grad_loadings: float32 [64, 16384], P(None, 'tm')
All inputs are finite; a program needn't handle non-finite values.
Results may differ from a plain program's by a relative error of at most 0.0021.
Values may be sent and summed in bfloat16 or wider, within the bound.
A program may use at most 128 MiB of HBM per device.

v0:
```python
import math
import jax
import jax.numpy as jnp
from jax import lax
from jax.sharding import PartitionSpec as P


def from_behind(block, axis, distance):
    devices = range(lax.axis_size(axis))
    route = [(i - distance, i) for i in devices if i - distance in devices]
    return lax.ppermute(block, axis, route)


def correlate(lhs, rhs, specs):
    return lax.conv_general_dilated(
        lhs, rhs, (1,), "VALID", dimension_numbers=specs, preferred_element_type=jnp.float32
    )


def forward_model(motifs, load_ext, time_len):
    reversed_load = load_ext[:, ::-1]
    result = correlate(reversed_load[None], motifs, ("NCH", "HIO", "NCH"))
    return result[0, :, :time_len][:, ::-1]


def backward_motif(motifs, res_ext, out_len):
    result = correlate(res_ext[None], motifs, ("NCH", "HOI", "NCH"))
    return result[0, :, :out_len]


def weight_term(reversed_load, reversed_res, piece_count):
    time_len = reversed_res.shape[1]
    window = lax.slice_in_dim(reversed_load, 0, piece_count + time_len - 1, axis=1)
    return correlate(window[:, None, :], reversed_res[:, None, :], ("NCH", "OIH", "HNC"))


def on_device(recording, motifs, loadings):
    lag_count = motifs.shape[0]
    motif_count = motifs.shape[1]
    neur_local = recording.shape[0]
    time_len = recording.shape[1]
    tm_count = lax.axis_size("tm")
    lag_share = lag_count // tm_count
    total_time = time_len * tm_count
    neurons = neur_local * lax.axis_size("neur")
    edge_cols = from_behind(loadings[:, time_len - lag_count :], "tm", 1)
    load_ext = jnp.concatenate([edge_cols, loadings], axis=1)
    rebuilt = forward_model(motifs, load_ext, time_len)
    residual = (rebuilt - recording.astype(jnp.float32)).astype(jnp.bfloat16)
    ahead_cols = from_behind(residual[:, :lag_count], "tm", -1)
    partial_value = backward_motif(
        motifs, jnp.concatenate([residual, ahead_cols], axis=1), time_len
    )
    grad_loadings = lax.psum(partial_value, "neur") * math.sqrt(motif_count / neurons)
    reversed_load = load_ext[:, ::-1]
    reversed_res = residual[:, ::-1]
    own_rows = lax.psum_scatter(
        weight_term(reversed_load, reversed_res, lag_share * lax.axis_size("tm")),
        "tm",
        scatter_dimension=0,
        tiled=True,
    )
    grad_motifs = own_rows * (1.0 / math.sqrt(total_time))
    return (grad_motifs, grad_loadings)


def solution(mesh):
    in_specs = (P("neur", "tm"), P(None, None, "neur"), P(None, "tm"))
    out_specs = (P("tm", None, "neur"), P(None, "tm"))
    return jax.shard_map(
        on_device, mesh=mesh, in_specs=in_specs, out_specs=out_specs, check_vma=False
    )
```

profile of v0, /device:TPU:0, one launch (start us, length us, event | category | flops | bytes accessed | tf_op | source)
XLA Modules:
  0.0 547.0 jit_solution(15876584063719561310)
XLA Ops:
  8.0 0.7 slice.18
  8.8 1.7 collective-permute-start
  10.4 1.1 copy.6
  11.5 0.3 collective-permute-done
  11.9 0.8 constant_dynamic-update-slice_fusion
  12.6 0.3 rev.10
  12.9 0.1 slice.24
  13.0 0.2 copy.5
  13.2 18.7 %fusion.4 = f32[1,512,256]{1,0,2:T(1,128)S(1)} fusion(bf16[1,64,384]{1,0,2:T(2,128)(2,1)S(1)} %copy.5, bf16[128,64,512]{2,1,0:T(8,128)(2,1)} %param.4), kind=kOutput, calls=%fused_computation.12 | convolution fusion | flops 2147483648 | bytes 8962048 | tf_op jit(solution)/shard_map/slice | solution.py:23
  31.9 0.3 rev.11
  32.3 0.3 rev.12
  32.6 0.3 reverse.1
  32.9 1.5 collective-permute-start.1
  34.4 0.1 slice_bitcast_fusion
  34.4 0.2 copy.7
  34.6 5.4 collective-permute-done.1
  40.0 24.7 %fusion = f32[1,64,256]{1,0,2:T(1,128)} fusion(bf16[128,64,512]{2,1,0:T(8,128)(2,1)} %param.4, bf16[1,512,384]{1,2,0:T(8,128)(2,1)S(1)} %maximum_bitcast_fusion), kind=kOutput, calls=%fused_computation | convolution fusion | flops 2147483648 | bytes 8847360 | tf_op jit(solution)/shard_map/slice | solution.py:28
  64.7 0.3 reduce-scatter.2.cloned.1.call-start
  65.0 19.4 %fusion.2 = f32[128,64,512]{2,1,0:T(8,128)} fusion(bf16[64,1,383]{0,1,2:T(2,128)(2,1)S(1)} %copy.7, bf16[512,1,256]{0,2,1:T(8,128)(2,1)S(1)} %bitcast.16), kind=kOutput, calls=%fused_computation.3 | convolution fusion | flops 2147483648 | bytes 17088384 | tf_op jit(solution)/shard_map/conv_general_dilated | solution.py:15
  84.4 33.6 %all-reduce.2.cloned.1.call-done = f32[64,256]{0,1:T(8,128)} async-done(((f32[64,256]{0,1:T(8,128)}), f32[64,256]{0,1:T(8,128)}) %all-reduce.2.cloned.1.call-update) | async-done | bytes 65552 | tf_op jit(solution)/shard_map/psum | solution.py:54
  118.0 0.9 broadcast_multiply_fusion.1
  119.0 0.7 copy.10
  119.7 418.2 %reduce-scatter.2.cloned.1.call-done = f32[2,64,512]{2,1,0:T(8,128)} async-done(((f32[128,64,512]{2,1,0:T(8,128)}), f32[2,64,512]{2,1,0:T(8,128)}) %reduce-scatter.2.cloned.1.call-update) | async-done | bytes 262160 | tf_op jit(solution)/shard_map/reduce_scatter | solution.py:57
  537.9 1.7 broadcast_multiply_fusion
  (8 shorter events, 0.2 us)
Async XLA Ops:
  8.0 110.0 %all-reduce.2.cloned.1.call-start = ((), (), s32[]{:S(2)}) async-start(), calls=%async_computation.2 | async-start | bytes 262144 | tf_op jit(solution)/shard_map/psum | solution.py:54
  8.8 3.1 collective-permute-start
  32.9 7.1 %collective-permute-start.1 = (bf16[512,128]{0,1:T(8,128)(2,1)S(1)}, bf16[512,128]{0,1:T(8,128)(2,1)S(1)}, u32[]{:S(2)}, u32[]{:S(2)}) collective-permute-start(bf16[512,128]{0,1:T(8,128)(2,1)S(1)} %slice.25), channel_id=1, source_target_pairs={{4,0},{8,4},{12,8},{16,12},{20,16},{24,20},{28,24},{32,28},{36,32}... | collective-permute-start | bytes 393224 | tf_op jit(solution)/shard_map/ppermute | solution.py:11
  64.7 473.1 %reduce-scatter.2.cloned.1.call-start = ((), (), s32[]{:S(2)}) async-start(), calls=%async_computation.1 | async-start | bytes 17039360 | tf_op jit(solution)/shard_map/reduce_scatter | solution.py:57
Sparse Core Ops, SparseCore 0:
  64.9 53.1 all-reduce.1
Sparse Core Ops, SparseCore 1:
  84.5 453.3 reduce-scatter.1
where the time goes:
time: 547 us
  waiting for transfers between devices  458 us (84%)
  matrix products  62.7 us (11%)
  between operations  15.6 us (3%)
    reduce_scatter x1, waiting for transfers between devices, on_device(): lax.psum_scatter(weight_term(reversed_load, reversed_res, lag_share * lax...  418 us
    psum x1, waiting for transfers between devices, on_device(): lax.psum(partial_value, 'neur') * math.sqrt(motif_count / neurons)  33.6 us
    slice x1, matrix products, backward_motif(): return result[0, :, :out_len]  24.7 us
    conv_general_dilated x1, matrix products, correlate(): lax.conv_general_dilated(lhs, rhs, (1,), 'VALID', dimension_numbers=specs...  19.4 us
    slice x1, matrix products, forward_model(): return result[0, :, :time_len][:, ::-1]  18.7 us
  transfers between devices with their start and end apart: 4, of which 4 were waited for; matrix products, arithmetic and copies ran while one was open for 4% of the time, Pallas kernels for 0%

commit v1 on v0

--- a/solution.py
+++ b/solution.py
@@ -51,7 +51,9 @@
     partial_value = backward_motif(
         motifs, jnp.concatenate([residual, ahead_cols], axis=1), time_len
     )
-    grad_loadings = lax.psum(partial_value, "neur") * math.sqrt(motif_count / neurons)
+    grad_loadings = jnp.sum(lax.all_gather(partial_value, "neur"), axis=0) * math.sqrt(
+        motif_count / neurons
+    )
     reversed_load = load_ext[:, ::-1]
     reversed_res = residual[:, ::-1]
     own_rows = lax.psum_scatter(

time: 547 us -> 517 us (0.945)
  waiting for transfers between devices: 458 us -> 416 us
  blocking collectives: 0 us -> 13.1 us
    psum x1 -> x0, waiting for transfers between devices: 33.6 us -> none  [on_device(): lax.psum(partial_value, 'neur') * math.sqrt(motif_count / neurons)]
    all_gather x0 -> x1, blocking collectives: none -> 13.1 us  [on_device(): lax.all_gather(partial_value, 'neur')]
    reduce_scatter x1, waiting for transfers between devices: 418 us -> 410 us  [on_device(): lax.psum_scatter(weight_term(reversed_load, reversed_res, lag_share * lax...]
  transfers between devices with their start and end apart: 4 -> 3, of which waited for: 4 -> 3; matrix products, arithmetic and copies ran while one was open for 4% -> 5% of each run, Pallas kernels for 0% -> 0%
where the time goes in v1:
time: 517 us
  waiting for transfers between devices  416 us (80%)
  matrix products  62.3 us (12%)
  between operations  14.2 us (3%)
  blocking collectives  13.1 us (3%)
  local copies, waits for them, and re-layouts  6.3 us (1%)
    reduce_scatter x1, waiting for transfers between devices, on_device(): lax.psum_scatter(weight_term(reversed_load, reversed_res, lag_share * lax...  410 us
    slice x1, matrix products, backward_motif(): return result[0, :, :out_len]  24 us
    conv_general_dilated x1, matrix products, correlate(): lax.conv_general_dilated(lhs, rhs, (1,), 'VALID', dimension_numbers=specs...  19.6 us
    slice x1, matrix products, forward_model(): return result[0, :, :time_len][:, ::-1]  18.7 us
    all_gather x1, blocking collectives, on_device(): lax.all_gather(partial_value, 'neur')  13.1 us
  transfers between devices with their start and end apart: 3, of which 3 were waited for; matrix products, arithmetic and copies ran while one was open for 5% of the time, Pallas kernels for 0%

profile of v1, /device:TPU:0, one launch (start us, length us, event | category | flops | bytes accessed | tf_op | source)
XLA Modules:
  0.0 516.7 jit_solution(16834507838326234762)
XLA Ops:
  7.2 0.7 slice.18
  7.9 1.7 collective-permute-start
  9.6 1.1 copy.11
  10.7 0.3 collective-permute-done
  11.0 0.8 constant_dynamic-update-slice_fusion
  11.8 0.3 rev.10
  12.1 0.1 slice.24
  12.2 0.3 reverse.1
  12.4 0.1 slice_bitcast_fusion
  12.5 0.2 copy.12
  12.7 0.2 copy.10
  12.9 18.7 %fusion.4 = f32[1,512,256]{1,0,2:T(1,128)S(1)} fusion(bf16[1,64,384]{1,0,2:T(2,128)(2,1)S(1)} %copy.10, bf16[128,64,512]{2,1,0:T(8,128)(2,1)} %param.4), kind=kOutput, calls=%fused_computation.12 | convolution fusion | flops 2147483648 | bytes 8962048 | tf_op jit(solution)/shard_map/slice | solution.py:23
  31.6 0.3 rev.11
  32.0 0.5 rev.12
  32.5 19.6 %fusion.2 = f32[128,64,512]{2,1,0:T(8,128)} fusion(bf16[64,1,383]{0,1,2:T(2,128)(2,1)S(1)} %copy.12, bf16[512,1,256]{0,2,1:T(8,128)(2,1)S(1)} %bitcast.15), kind=kOutput, calls=%fused_computation.3 | convolution fusion | flops 2147483648 | bytes 17088384 | tf_op jit(solution)/shard_map/conv_general_dilated | solution.py:15
  52.1 0.9 copy-done.1
  53.1 1.3 collective-permute-start.1
  54.4 5.8 %collective-permute-done.1 = bf16[512,128]{0,1:T(8,128)(2,1)S(1)} collective-permute-done((bf16[512,128]{0,1:T(8,128)(2,1)S(1)}, bf16[512,128]{0,1:T(8,128)(2,1)S(1)}, u32[]{:S(2)}, u32[]{:S(2)}) %collective-permute-start.1) | collective-permute-done | bytes 131104 | tf_op jit(solution)/shard_map/ppermute | solution.py:11
  60.2 24.0 %fusion = f32[1,64,256]{1,0,2:T(1,128)S(1)} fusion(bf16[128,64,512]{2,1,0:T(8,128)(2,1)} %param.4, bf16[1,512,384]{1,2,0:T(8,128)(2,1)S(1)} %maximum_bitcast_fusion), kind=kOutput, calls=%fused_computation | convolution fusion | flops 2147483648 | bytes 8847360 | tf_op jit(solution)/shard_map/slice | solution.py:28
  84.4 13.1 %all_gather.3 = f32[4,64,256]{2,1,0:T(8,128)S(1)} all-gather(f32[1,64,256]{2,1,0:T(8,128)S(1)} %copy.15), channel_id=1, replica_groups=mesh['tm'=64,'neur'=4] {'neur'}, dimensions={0}, use_global_device_ids=true | all-gather | bytes 327680 | tf_op jit(solution)/shard_map/all_gather | solution.py:54
  97.5 0.1 copy.19
  97.6 0.7 copy.17
  98.3 409.9 %reduce-scatter.2.cloned.1.call-done = f32[2,64,512]{2,1,0:T(8,128)} async-done(((f32[128,64,512]{2,1,0:T(8,128)}), f32[2,64,512]{2,1,0:T(8,128)}) %reduce-scatter.2.cloned.1.call-update) | async-done | bytes 262160 | tf_op jit(solution)/shard_map/reduce_scatter | solution.py:59
  508.2 1.7 broadcast_multiply_fusion
  (13 shorter events, 0.3 us)
Async XLA Ops:
  7.2 501.0 %reduce-scatter.2.cloned.1.call-start = ((), (), s32[]{:S(2)}) async-start(), calls=%async_computation.1 | async-start | bytes 17039360 | tf_op jit(solution)/shard_map/reduce_scatter | solution.py:59
  7.9 3.1 collective-permute-start
  32.0 20.1 %copy-start = (bf16[512,256]{0,1:T(8,128)(2,1)}, bf16[512,256]{0,1:T(8,128)(2,1)S(1)}, u32[]{:S(2)}) copy-start(bf16[512,256]{0,1:T(8,128)(2,1)S(1)} %subtract_convert_fusion) | copy-start | bytes 786436
  52.1 1.0 copy-start.1
  53.1 7.1 %collective-permute-start.1 = (bf16[512,128]{0,1:T(8,128)(2,1)S(1)}, bf16[512,128]{0,1:T(8,128)(2,1)S(1)}, u32[]{:S(2)}, u32[]{:S(2)}) collective-permute-start(bf16[512,128]{0,1:T(8,128)(2,1)S(1)} %slice.25), channel_id=1, source_target_pairs={{4,0},{8,4},{12,8},{16,12},{20,16},{24,20},{28,24},{32,28},{36,32}... | collective-permute-start | bytes 393224 | tf_op jit(solution)/shard_map/ppermute | solution.py:11
Sparse Core Ops, SparseCore 0:
  52.3 455.8 reduce-scatter.1
